TPU v7x, 32 devices: a whole 2x2x4 slice. The times are simulated.
32 devices in a mesh: particle: 2 (over x), coil: 8 (over z, y), phase: 2 (over core).
Axes of the slice: x: 2, y: 2, z: 4, core: 2. Of those that a mesh axis runs over, the one named last changes fastest.
Arguments:
- position: float32 [256, 16, 4, 384], P('coil', 'phase', 'particle'), parts along dimension 2, may hold values from -6 to 6
- coil_maps: bfloat16 [8, 256, 4, 384], P('coil', None, 'particle'), parts along dimension 2, may hold values from -2 to 2
- kspace_data: bfloat16 [8, 256, 16, 4, 384], P('coil', None, 'phase', 'particle'), parts along dimension 3, may hold values from -1.796875 to 1.796875
- sample_mask: int32 [256, 16], P(None, 'phase'), may hold values 0 or 1
Outputs:
- gradient: float32 [256, 16, 4, 384], P('coil', 'phase', 'particle'), parts along dimension 2
There are 2 independent parts, one for each index of `particle`. A program takes and returns all parts, laid end to end along the dimension named above; an argument that names none is the same for every part. Nothing has to cross between parts.
All inputs are finite; a program needn't handle non-finite values. No bound on the sum of `sample_mask` on one device may be relied on, other than what follows from the above.
Results may differ from a plain program's by a relative error of at most 0.0012.
Values may be sent and summed in bfloat16 or wider, within the bound.
A program may use at most 64 MiB of HBM per device.

v0:
```python
import math

import jax
import jax.numpy as jnp
from jax import lax
from jax.sharding import PartitionSpec as P


def with_halo(block, sides, width):
    for axis, dim in sides:
        count = lax.axis_size(axis)
        forward = [(i, i + 1) for i in range(count - 1)]
        forward.append((count - 1, 0))
        backward = [(target, source) for source, target in forward]
        low = lax.ppermute(
            lax.slice_in_dim(block, block.shape[dim] - width, None, axis=dim), axis, forward
        )
        high = lax.ppermute(lax.slice_in_dim(block, 0, width, axis=dim), axis, backward)
        block = jnp.concatenate([low, block, high], axis=dim)
    return block


def dft_tables(length):
    counter = jnp.arange(length, dtype=jnp.int32)
    product = counter[:, None] * counter[None, :] % length
    angles = product.astype(jnp.float32) * (2.0 * math.pi / length)
    scaling = 1.0 / math.sqrt(length)
    return (jnp.cos(angles) * scaling, -jnp.sin(angles) * scaling)


def build_tables(rows_total, width):
    row_real, row_imag = dft_tables(rows_total)
    col_real, col_imag = dft_tables(width)
    forward_wide = jnp.concatenate(
        [jnp.concatenate([col_real, col_imag], 1), jnp.concatenate([-col_imag, col_real], 1)], 0
    )
    backward_wide = jnp.concatenate(
        [jnp.concatenate([col_real, -col_imag], 1), jnp.concatenate([col_imag, col_real], 1)], 0
    )
    return (
        row_real.astype(jnp.bfloat16),
        row_imag.astype(jnp.bfloat16),
        forward_wide.astype(jnp.bfloat16),
        backward_wide.astype(jnp.bfloat16),
    )


def complex_times(factor, values, conjugate):
    width = values.shape[-1] // 2
    factor_real = factor[..., :width]
    factor_imag = factor[..., width:]
    if conjugate:
        factor_imag = -factor_imag
    value_real = values[..., :width]
    value_imag = values[..., width:]
    out_real = factor_real * value_real - factor_imag * value_imag
    out_imag = factor_real * value_imag + factor_imag * value_real
    return jnp.concatenate([out_real, out_imag], -1)


def rows_apply(table_real, table_imag, values, adjoint):
    width = values.shape[-1] // 2
    real_part = jnp.einsum("kn,npsd->kpsd", table_real, values, preferred_element_type=jnp.float32)
    imag_part = jnp.einsum("kn,npsd->kpsd", table_imag, values, preferred_element_type=jnp.float32)
    if adjoint:
        out_real = real_part[..., :width] + imag_part[..., width:]
        out_imag = real_part[..., width:] - imag_part[..., :width]
    else:
        out_real = real_part[..., :width] - imag_part[..., width:]
        out_imag = real_part[..., width:] + imag_part[..., :width]
    return jnp.concatenate([out_real, out_imag], -1)


def local(position, coil_maps, kspace_data, sample_mask):
    rows_here = position.shape[0]
    rows_total = coil_maps.shape[1]
    width = position.shape[3] // 2
    row_real, row_imag, forward_wide, backward_wide = build_tables(rows_total, width)
    coil_map = coil_maps[0]
    coil_data = kspace_data[0]
    sample_weight = sample_mask.astype(jnp.float32)[:, :, None, None]
    position_low = position.astype(jnp.bfloat16)
    map_rows = coil_map.astype(jnp.float32)[:, None]
    lifted = complex_times(
        map_rows,
        lax.all_gather(position_low, "coil", axis=0, tiled=True).astype(jnp.float32),
        False,
    ).astype(jnp.bfloat16)
    spread = jnp.einsum(
        "npsc,cd->npsd", lifted, forward_wide, preferred_element_type=jnp.float32
    ).astype(jnp.bfloat16)
    kspace = rows_apply(row_real, row_imag, spread, False)
    residual = (sample_weight * (kspace - coil_data.astype(jnp.float32))).astype(jnp.bfloat16)
    back_rows = rows_apply(row_real, row_imag, residual, True).astype(jnp.bfloat16)
    back = jnp.einsum("npsc,cd->npsd", back_rows, backward_wide, preferred_element_type=jnp.float32)
    map_rows = coil_map.astype(jnp.float32)[:, None]
    summed = lax.psum(complex_times(map_rows, back, True), "coil")
    likelihood = lax.dynamic_slice_in_dim(summed, lax.axis_index("coil") * rows_here, rows_here, 0)
    padded = with_halo(position, (("coil", 0), ("phase", 1)), 1)
    phase_part = 2.0 * position - padded[1:-1, :-2] - padded[1:-1, 2:]
    row_part = 2.0 * position - padded[:-2, 1:-1] - padded[2:, 1:-1]
    return 0.6 * likelihood + 0.5 * phase_part + 0.3 * row_part


def solution(mesh):
    in_specs = (
        P("coil", "phase", "particle", None),
        P("coil", None, "particle", None),
        P("coil", None, "phase", "particle", None),
        P(None, "phase"),
    )
    out_specs = P("coil", "phase", "particle", None)
    return jax.shard_map(local, mesh=mesh, in_specs=in_specs, out_specs=out_specs, check_vma=False)
```

profile of v0, /device:TPU:0, one launch (start us, length us, event | category | flops | bytes accessed | tf_op | source)
XLA Modules:
  0.0 333.7 jit_solution(8550984614529454720)
XLA Ops:
  6.5 0.0 copy-start.4
  6.5 0.0 all-gather.2.cloned.1.call-start
  6.5 2.1 copy.23
  8.7 0.0 all-gather.2.cloned.1.call-update
  8.7 0.0 all-reduce.2.cloned.1.call-start
  8.8 1.3 bitcast_convert_fusion
  10.0 0.7 negate_bitcast_fusion
  10.8 0.0 copy-start
  10.9 0.0 copy-done.4
  10.9 0.9 copy.9
  11.8 0.8 fusion.44
  12.6 0.8 negate_convert_fusion
  13.4 58.9 %all-gather.2.cloned.1.call-done = bf16[256,8,2,384]{3,0,2,1:T(8,128)(2,1)} async-done(((bf16[32,8,2,384]{3,0,2,1:T(8,128)(2,1)}), bf16[256,8,2,384]{3,0,2,1:T(8,128)(2,1)}) %all-gather.2.cloned.1.call-update) | async-done | bytes 3145744 | tf_op jit(solution)/shard_map/all_gather | solution.py:86
  72.3 2.5 convert_element_type.81
  74.9 0.0 copy-done
  74.9 1.8 subtract_convert_fusion
  76.7 2.3 fusion.12
  79.0 1.9 fusion.49
  80.9 4.6 %fusion.53 = f32[256,8,2,384]{3,0,2,1:T(8,128)} fusion(bf16[256,8,2,384]{3,0,2,1:T(8,128)(2,1)S(1)} %fusion.12), kind=kOutput, calls=%fused_computation.82 | convolution fusion | flops 806354944 | bytes 9437184 | tf_op jit(solution)/shard_map/kn,npsd->kpsd/dot_general | solution.py:63
  85.4 9.2 %slice_subtract_fusion.1 = (f32[256,8,2,192]{3,0,2,1:T(8,128)}, f32[256,8,2,192]{3,0,2,1:T(8,128)}) fusion(f32[256,8,2,384]{3,0,2,1:T(8,128)S(1)} %fusion.49, f32[256,8,2,384]{3,0,2,1:T(8,128)} %fusion.53), kind=kLoop, calls=%fused_computation.9 | loop fusion | flops 1572864 | bytes 18874368 | tf_op jit(solution)/shard_map/sub | solution.py:69
  94.7 5.3 %fusion.1 = bf16[256,8,2,384]{3,0,2,1:T(8,128)(2,1)S(1)} fusion(f32[256,8,2,192]{3,0,2,1:T(8,128)} %get-tuple-element.8, f32[256,8,2,192]{3,0,2,1:T(8,128)} %get-tuple-element.7, bf16[1,256,8,2,384]{4,3,2,1,0:T(2,128)(2,1)} %param.6, f32[256,8]{0,1:T(8,128)S(1)} %convert_element_type.79), kind=kLoop, calls=%fused_computation.2 | loop fusion | flops 7864320 | bytes 12591104 | tf_op jit(solution)/shard_map/convert_element_type | solution.py:93
  100.0 1.9 fusion.47
  101.9 1.9 fusion.51
  103.8 2.6 fusion.3
  106.4 0.0 copy-start.1
  106.4 0.0 copy-start.3
  106.4 2.3 fusion.8
  108.7 0.0 copy-done.1
  108.7 0.0 copy-done.3
  108.7 2.0 multiply_subtract_fusion
  110.8 3.9 %pad_maximum_fusion = f32[256,8,2,384]{3,0,2,1:T(8,128)} fusion(f32[256,8,2,192]{3,0,2,1:T(8,128)S(1)} %get-tuple-element.10, f32[256,8,2,192]{3,0,2,1:T(8,128)S(1)} %get-tuple-element.9), kind=kLoop, calls=%fused_computation.3 | loop fusion | flops 1572864 | bytes 12582912 | tf_op jit(solution)/shard_map/concatenate | solution.py:58
  114.7 0.0 copy-start.2
  114.7 0.0 all-reduce.2.cloned.1.call-update
  114.7 1.1 copy-done.2
  115.9 0.6 collective-permute-start
  116.5 4.2 %collective-permute-start.1 = (f32[1,8,2,384]{3,0,2,1:T(1,128)S(1)}, f32[1,8,2,384]{3,0,2,1:T(1,128)S(1)}, u32[]{:S(2)}, u32[]{:S(2)}) collective-permute-start(f32[1,8,2,384]{3,0,2,1:T(1,128)S(1)} %copy.12), channel_id=1, source_target_pairs={{2,0},{4,2},{6,4},{8,6},{10,8},{12,10},{14,12},{0,14},{3,1},{5,3},... | collective-permute-start | bytes 73736 | tf_op jit(solution)/shard_map/ppermute | solution.py:18
  120.7 0.3 copy.6
  121.0 1.6 collective-permute-done
  122.5 0.2 collective-permute-done.1
  122.8 0.1 collective-permute-start.2
  122.8 0.5 collective-permute-start.3
  123.3 0.8 collective-permute-done.2
  124.2 0.2 collective-permute-done.3
  124.3 199.5 %all-reduce.2.cloned.1.call-done = f32[256,8,2,384]{3,0,2,1:T(8,128)} async-done(((f32[256,8,2,384]{3,0,2,1:T(8,128)}), f32[256,8,2,384]{3,0,2,1:T(8,128)}) %all-reduce.2.cloned.1.call-update) | async-done | bytes 6291472 | tf_op jit(solution)/shard_map/psum | solution.py:97
  323.8 1.6 fusion.17
  325.4 1.5 copy.16
  (7 shorter events, 0.2 us)
Async XLA Ops:
  6.5 4.3 %copy-start.4 = (s32[256,8]{0,1:T(8,128)S(1)}, s32[256,8]{0,1:T(8,128)}, u32[]{:S(2)}) copy-start(s32[256,8]{0,1:T(8,128)} %param.7) | copy-start | bytes 24580
  6.5 65.8 %all-gather.2.cloned.1.call-start = ((), (), s32[]{:S(2)}) async-start(), calls=%async_computation | async-start | bytes 3538944 | tf_op jit(solution)/shard_map/all_gather | solution.py:86
  8.7 315.1 %all-reduce.2.cloned.1.call-start = ((), (), s32[]{:S(2)}) async-start(), calls=%async_computation.1 | async-start | bytes 12582912 | tf_op jit(solution)/shard_map/psum | solution.py:97
  10.8 64.0 %copy-start = (f32[256,2,192]{2,0,1:T(8,128)}, f32[256,2,192]{2,0,1:T(8,128)S(1)}, u32[]{:S(2)}) copy-start(f32[256,2,192]{2,0,1:T(8,128)S(1)} %copy.5) | copy-start | bytes 1179652
  106.4 2.3 copy-start.1
  106.4 2.3 copy-start.3
  114.7 1.1 copy-start.2
  115.9 6.7 %collective-permute-start = (f32[1,8,2,384]{3,0,2,1:T(1,128)S(1)}, f32[1,8,2,384]{3,0,2,1:T(1,128)S(1)}, u32[]{:S(2)}, u32[]{:S(2)}) collective-permute-start(f32[1,8,2,384]{3,0,2,1:T(1,128)S(1)} %copy.11), channel_id=1, source_target_pairs={{0,2},{2,4},{4,6},{6,8},{8,10},{10,12},{12,14},{14,0},{1,3},{3,5},... | collective-permute-start | bytes 73736 | tf_op jit(solution)/shard_map/ppermute | solution.py:15
  116.5 6.2 %collective-permute-start.1 = (f32[1,8,2,384]{3,0,2,1:T(1,128)S(1)}, f32[1,8,2,384]{3,0,2,1:T(1,128)S(1)}, u32[]{:S(2)}, u32[]{:S(2)}) collective-permute-start(f32[1,8,2,384]{3,0,2,1:T(1,128)S(1)} %copy.12), channel_id=1, source_target_pairs={{2,0},{4,2},{6,4},{8,6},{10,8},{12,10},{14,12},{0,14},{3,1},{5,3},... | collective-permute-start | bytes 73736 | tf_op jit(solution)/shard_map/ppermute | solution.py:18
  122.8 1.4 collective-permute-start.2
  122.8 1.5 collective-permute-start.3
Sparse Core Ops, SparseCore 0:
  9.5 62.7 all-gather.1
  114.8 208.9 all-reduce.1
where the time goes:
time: 334 us
  waiting for transfers between devices  261 us (78%)
  other arithmetic  32.7 us (10%)
  matrix products  14.8 us (4%)
  between operations  13.6 us (4%)
  local copies, waits for them, and re-layouts  6.04 us (2%)
  starting transfers between devices  5.44 us (2%)
    psum x1, waiting for transfers between devices, local(): summed = lax.psum(complex_times(map_rows, back, True), 'coil')  199 us
    all_gather x1, waiting for transfers between devices, local(): lax.all_gather(position_low, 'coil', axis=0, tiled=True).astype(jnp.float32)  58.9 us
    sub x1, other arithmetic, rows_apply(): out_real = real_part[..., :width] - imag_part[..., width:]  9.23 us
  transfers between devices with their start and end apart: 6, of which 6 were waited for; matrix products, arithmetic and copies ran while one was open for 1% of the time, Pallas kernels for 0%

commit v1 on v0

--- a/solution.py
+++ b/solution.py
@@ -72,7 +72,6 @@
 
 
 def local(position, coil_maps, kspace_data, sample_mask):
-    rows_here = position.shape[0]
     rows_total = coil_maps.shape[1]
     width = position.shape[3] // 2
     row_real, row_imag, forward_wide, backward_wide = build_tables(rows_total, width)
@@ -94,8 +93,8 @@
     back_rows = rows_apply(row_real, row_imag, residual, True).astype(jnp.bfloat16)
     back = jnp.einsum("npsc,cd->npsd", back_rows, backward_wide, preferred_element_type=jnp.float32)
     map_rows = coil_map.astype(jnp.float32)[:, None]
-    summed = lax.psum(complex_times(map_rows, back, True), "coil")
-    likelihood = lax.dynamic_slice_in_dim(summed, lax.axis_index("coil") * rows_here, rows_here, 0)
+    partial = complex_times(map_rows, back, True).astype(jnp.bfloat16)
+    likelihood = lax.psum_scatter(partial, "coil", scatter_dimension=0, tiled=True).astype(jnp.float32)
     padded = with_halo(position, (("coil", 0), ("phase", 1)), 1)
     phase_part = 2.0 * position - padded[1:-1, :-2] - padded[1:-1, 2:]
     row_part = 2.0 * position - padded[:-2, 1:-1] - padded[2:, 1:-1]

time: 334 us -> 197 us (0.59)
  waiting for transfers between devices: 261 us -> 126 us
    psum x1 -> x0, waiting for transfers between devices: 199 us -> none  [local(): summed = lax.psum(complex_times(map_rows, back, True), 'coil')]
    reduce_scatter x0 -> x1, waiting for transfers between devices: none -> 64.9 us  [local(): lax.psum_scatter(partial, 'coil', scatter_dimension=0, tiled=True)]
    another operation x4 -> x5, other arithmetic: 6.02 us -> 7.84 us
  transfers between devices with their start and end apart: 6 -> 6, of which waited for: 6 -> 5; matrix products, arithmetic and copies ran while one was open for 1% -> 3% of each run, Pallas kernels for 0% -> 0%
where the time goes in v1:
time: 197 us; the launch traced here: 196 us
  waiting for transfers between devices  126 us (64%)
  other arithmetic  31.3 us (16%)
  matrix products  14.8 us (8%)
  between operations  13.6 us (7%)
  starting transfers between devices  5.44 us (3%)
  local copies, waits for them, and re-layouts  4.94 us (3%)
    reduce_scatter x1, waiting for transfers between devices, local(): lax.psum_scatter(partial, 'coil', scatter_dimension=0, tiled=True)  64.9 us
    all_gather x1, waiting for transfers between devices, local(): lax.all_gather(position_low, 'coil', axis=0, tiled=True).astype(jnp.float32)  58.9 us
    sub x1, other arithmetic, rows_apply(): out_real = real_part[..., :width] - imag_part[..., width:]  9.23 us
    another operation x5, other arithmetic  7.84 us
    dot_general x2, matrix products, rows_apply(): jnp.einsum('kn,npsd->kpsd', table_real, values, preferred_element_type=jn...  6.45 us
    convert_element_type x1, other arithmetic, local(): (sample_weight * (kspace - coil_data.astype(jnp.float32))).astype(jnp.bfl...  5.32 us
    ppermute x2, starting transfers between devices, with_halo(): lax.ppermute(lax.slice_in_dim(block, 0, width, axis=dim), axis, backward)  4.71 us
  transfers between devices with their start and end apart: 6, of which 5 were waited for; matrix products, arithmetic and copies ran while one was open for 3% of the time, Pallas kernels for 0%

profile of v1, /device:TPU:0, one launch (start us, length us, event | category | flops | bytes accessed | tf_op | source)
XLA Modules:
  0.0 196.4 jit_solution(1061653901365311460)
XLA Ops:
  6.5 0.0 copy-start.4
  6.5 0.0 all-gather.2.cloned.1.call-start
  6.5 2.1 %copy.23 = bf16[32,8,2,384]{3,0,2,1:T(8,128)(2,1)} copy(f32[32,8,2,384]{3,2,1,0:T(2,128)} %param.4) | data formatting | bytes 1179648 | tf_op args[0]
  8.7 0.0 all-gather.2.cloned.1.call-update
  8.7 0.0 reduce-scatter.2.cloned.1.call-start
  8.8 1.3 bitcast_convert_fusion
  10.0 0.7 negate_bitcast_fusion
  10.8 0.0 copy-start
  10.9 0.0 copy-done.4
  10.9 0.9 copy.9
  11.8 0.8 fusion.44
  12.6 0.8 negate_convert_fusion
  13.4 58.9 %all-gather.2.cloned.1.call-done = bf16[256,8,2,384]{3,0,2,1:T(8,128)(2,1)} async-done(((bf16[32,8,2,384]{3,0,2,1:T(8,128)(2,1)}), bf16[256,8,2,384]{3,0,2,1:T(8,128)(2,1)}) %all-gather.2.cloned.1.call-update) | async-done | bytes 3145744 | tf_op jit(solution)/shard_map/all_gather | solution.py:85
  72.3 2.5 %convert_element_type.85 = f32[256,8,2,384]{3,0,2,1:T(8,128)S(1)} convert(bf16[256,8,2,384]{3,0,2,1:T(8,128)(2,1)} %all-gather.2.cloned.1.call-done) | non-fusion elementwise | flops 1572864 | bytes 9437184 | tf_op jit(solution)/shard_map/convert_element_type | solution.py:85
  74.9 0.0 copy-done
  74.9 1.8 subtract_convert_fusion.1
  76.7 2.3 %fusion.12 = bf16[256,8,2,384]{3,0,2,1:T(8,128)(2,1)S(1)} fusion(bf16[256,8,2,192]{3,0,2,1:T(8,128)(2,1)S(1)} %get-tuple-element.12, bf16[256,8,2,192]{3,0,2,1:T(8,128)(2,1)S(1)} %get-tuple-element.11, bf16[192,192]{1,0:T(8,128)(2,1)S(1)} %get-tuple-element.21, bf16[192,192]{1,0:T(8,128)(2,1)S(1)} %get-tuple-element.20, bf16[192,192]{1,0:T(8,128)(2,1)S(1)} %fusion.44), kind=kOutput, calls=%fused_computation.22 | convolution fusion | flops 1217003520 | bytes 6512640 | tf_op jit(solution)/shard_map/npsc,cd->npsd/dot_general | solution.py:88
  79.0 1.9 fusion.49
  80.9 4.6 %fusion.53 = f32[256,8,2,384]{3,0,2,1:T(8,128)} fusion(bf16[256,8,2,384]{3,0,2,1:T(8,128)(2,1)S(1)} %fusion.12), kind=kOutput, calls=%fused_computation.82 | convolution fusion | flops 806354944 | bytes 9437184 | tf_op jit(solution)/shard_map/kn,npsd->kpsd/dot_general | solution.py:63
  85.4 9.2 %slice_subtract_fusion.1 = (f32[256,8,2,192]{3,0,2,1:T(8,128)}, f32[256,8,2,192]{3,0,2,1:T(8,128)}) fusion(f32[256,8,2,384]{3,0,2,1:T(8,128)S(1)} %fusion.49, f32[256,8,2,384]{3,0,2,1:T(8,128)} %fusion.53), kind=kLoop, calls=%fused_computation.8 | loop fusion | flops 1572864 | bytes 18874368 | tf_op jit(solution)/shard_map/sub | solution.py:69
  94.7 5.3 %fusion.1 = bf16[256,8,2,384]{3,0,2,1:T(8,128)(2,1)S(1)} fusion(f32[256,8,2,192]{3,0,2,1:T(8,128)} %get-tuple-element.8, f32[256,8,2,192]{3,0,2,1:T(8,128)} %get-tuple-element.7, bf16[1,256,8,2,384]{4,3,2,1,0:T(2,128)(2,1)} %param.6, f32[256,8]{0,1:T(8,128)S(1)} %convert_element_type.83), kind=kLoop, calls=%fused_computation.2 | loop fusion | flops 7864320 | bytes 12591104 | tf_op jit(solution)/shard_map/convert_element_type | solution.py:92
  100.0 1.9 fusion.47
  101.9 1.9 fusion.51
  103.8 2.6 %fusion.3 = (bf16[256,8,2,192]{3,0,2,1:T(8,128)(2,1)S(1)}, bf16[256,8,2,192]{3,0,2,1:T(8,128)(2,1)S(1)}) fusion(f32[256,8,2,384]{3,0,2,1:T(8,128)S(1)} %fusion.47, f32[256,8,2,384]{3,0,2,1:T(8,128)S(1)} %fusion.51), kind=kLoop, calls=%fused_computation.6 | loop fusion | flops 3145728 | bytes 15728640 | tf_op jit(solution)/shard_map/convert.10
  106.4 0.0 copy-start.1
  106.4 0.0 copy-start.3
  106.4 2.3 %fusion.8 = f32[256,8,2,384]{3,0,2,1:T(8,128)S(1)} fusion(bf16[256,8,2,192]{3,0,2,1:T(8,128)(2,1)S(1)} %get-tuple-element.6, bf16[256,8,2,192]{3,0,2,1:T(8,128)(2,1)S(1)} %get-tuple-element.5, bf16[192,192]{1,0:T(8,128)(2,1)S(1)} %get-tuple-element.21, bf16[192,192]{1,0:T(8,128)(2,1)S(1)} %fusion.44, bf16[192,192]{1,0:T(8,128)(2,1)S(1)} %get-tuple-element.20), kind=kOutput, calls=%fused_computation.17 | convolution fusion | flops 1215430656 | bytes 9658368 | tf_op jit(solution)/shard_map/npsc,cd->npsd/dot_general | solution.py:94
  108.7 0.0 copy-done.1
  108.7 0.0 copy-done.3
  108.7 1.8 subtract_convert_fusion
  110.6 0.0 copy-start.2
  110.6 2.8 %pad_maximum_fusion = bf16[256,8,2,384]{3,0,2,1:T(8,128)(2,1)} fusion(bf16[256,8,2,192]{3,0,2,1:T(8,128)(2,1)S(1)} %get-tuple-element.10, bf16[256,8,2,192]{3,0,2,1:T(8,128)(2,1)S(1)} %get-tuple-element.9), kind=kLoop, calls=%fused_computation.21 | loop fusion | flops 6291456 | bytes 6291456 | tf_op jit(solution)/shard_map/concatenate | solution.py:58
  113.4 0.0 reduce-scatter.2.cloned.1.call-update
  113.4 0.0 copy-done.2
  113.5 0.6 collective-permute-start
  114.1 4.2 %collective-permute-start.1 = (f32[1,8,2,384]{3,0,2,1:T(1,128)S(1)}, f32[1,8,2,384]{3,0,2,1:T(1,128)S(1)}, u32[]{:S(2)}, u32[]{:S(2)}) collective-permute-start(f32[1,8,2,384]{3,0,2,1:T(1,128)S(1)} %copy.12), channel_id=1, source_target_pairs={{2,0},{4,2},{6,4},{8,6},{10,8},{12,10},{14,12},{0,14},{3,1},{5,3},... | collective-permute-start | bytes 73736 | tf_op jit(solution)/shard_map/ppermute | solution.py:18
  118.4 0.3 copy.6
  118.6 1.5 collective-permute-done
  120.1 0.0 collective-permute-done.1
  120.1 0.1 collective-permute-start.2
  120.2 0.5 collective-permute-start.3
  120.7 0.8 collective-permute-done.2
  121.5 0.2 collective-permute-done.3
  121.7 64.9 %reduce-scatter.2.cloned.1.call-done = bf16[32,8,2,384]{3,0,2,1:T(8,128)(2,1)} async-done(((bf16[256,8,2,384]{3,0,2,1:T(8,128)(2,1)}), bf16[32,8,2,384]{3,0,2,1:T(8,128)(2,1)}) %reduce-scatter.2.cloned.1.call-update) | async-done | bytes 393232 | tf_op jit(solution)/shard_map/reduce_scatter | solution.py:97
  186.6 1.5 fusion.17
  188.1 1.5 copy.16
  (7 shorter events, 0.2 us)
Async XLA Ops:
  6.5 4.3 %copy-start.4 = (s32[256,8]{0,1:T(8,128)S(1)}, s32[256,8]{0,1:T(8,128)}, u32[]{:S(2)}) copy-start(s32[256,8]{0,1:T(8,128)} %param.7) | copy-start | bytes 24580
  6.5 65.8 %all-gather.2.cloned.1.call-start = ((), (), s32[]{:S(2)}) async-start(), calls=%async_computation.1 | async-start | bytes 3538944 | tf_op jit(solution)/shard_map/all_gather | solution.py:85
  8.7 177.9 %reduce-scatter.2.cloned.1.call-start = ((), (), s32[]{:S(2)}) async-start(), calls=%async_computation.2 | async-start | bytes 3538944 | tf_op jit(solution)/shard_map/reduce_scatter | solution.py:97
  10.8 64.0 %copy-start = (f32[256,2,192]{2,0,1:T(8,128)}, f32[256,2,192]{2,0,1:T(8,128)S(1)}, u32[]{:S(2)}) copy-start(f32[256,2,192]{2,0,1:T(8,128)S(1)} %copy.5) | copy-start | bytes 1179652
  106.4 2.3 %copy-start.1 = (f32[256,2,192]{2,0,1:T(8,128)S(1)}, f32[256,2,192]{2,0,1:T(8,128)}, u32[]{:S(2)}) copy-start(f32[256,2,192]{2,0,1:T(8,128)} %copy-done) | copy-start | bytes 1179652
  106.4 2.3 %copy-start.3 = (f32[256,2,192]{2,0,1:T(8,128)S(1)}, f32[256,2,192]{2,0,1:T(8,128)}, u32[]{:S(2)}) copy-start(f32[256,2,192]{2,0,1:T(8,128)} %copy.9) | copy-start | bytes 1179652
  110.6 2.9 %copy-start.2 = (f32[32,8,2,384]{3,2,1,0:T(2,128)S(1)}, f32[32,8,2,384]{3,2,1,0:T(2,128)}, u32[]{:S(2)}) copy-start(f32[32,8,2,384]{3,2,1,0:T(2,128)} %param.4) | copy-start | bytes 2359300
  113.5 6.6 %collective-permute-start = (f32[1,8,2,384]{3,0,2,1:T(1,128)S(1)}, f32[1,8,2,384]{3,0,2,1:T(1,128)S(1)}, u32[]{:S(2)}, u32[]{:S(2)}) collective-permute-start(f32[1,8,2,384]{3,0,2,1:T(1,128)S(1)} %copy.11), channel_id=1, source_target_pairs={{0,2},{2,4},{4,6},{6,8},{8,10},{10,12},{12,14},{14,0},{1,3},{3,5},... | collective-permute-start | bytes 73736 | tf_op jit(solution)/shard_map/ppermute | solution.py:15
  114.1 6.0 %collective-permute-start.1 = (f32[1,8,2,384]{3,0,2,1:T(1,128)S(1)}, f32[1,8,2,384]{3,0,2,1:T(1,128)S(1)}, u32[]{:S(2)}, u32[]{:S(2)}) collective-permute-start(f32[1,8,2,384]{3,0,2,1:T(1,128)S(1)} %copy.12), channel_id=1, source_target_pairs={{2,0},{4,2},{6,4},{8,6},{10,8},{12,10},{14,12},{0,14},{3,1},{5,3},... | collective-permute-start | bytes 73736 | tf_op jit(solution)/shard_map/ppermute | solution.py:18
  120.1 1.4 collective-permute-start.2
  120.2 1.5 collective-permute-start.3
Sparse Core Ops, SparseCore 0:
  9.5 62.7 all-gather.1
  113.6 73.0 reduce-scatter.1
